TPU v7x, 32 devices: a whole 2x2x4 slice. The times are simulated.
32 devices in a mesh: dp: 4 (over y, x), ctx: 8 (over z, core).
Axes of the slice: x: 2, y: 2, z: 4, core: 2. Of those that a mesh axis runs over, the one named last changes fastest.
Arguments:
- tokens: bfloat16 [4, 1024, 1536], P('dp', 'ctx'), may hold values from -6 to 6
- positions: int32 [4, 1024], P('dp', 'ctx'), may hold values from 0 to 3071, as said below
- block_order: int32 [16], replicated, may hold values from 0 to 15, as said below
- cotangent: bfloat16 [4, 1024, 1536], P('dp', 'ctx'), may hold values from -6 to 6
- gain_attn: bfloat16 [1536], P('dp'), may hold values from 0.099609375 to 1.8984375
- w_qkv: bfloat16 [1536, 2048], P('dp'), may hold values from -0.15625 to 0.15625
- b_qkv: bfloat16 [2048], P('dp'), may hold values from -3 to 3
- w_out: bfloat16 [1536, 1536], P('dp'), may hold values from -1.75 to 1.75
- gain_mlp: bfloat16 [1536], P('dp'), may hold values from 0.099609375 to 1.8984375
- w_gate: bfloat16 [1536, 8960], P('dp'), may hold values from -0.15625 to 0.15625
- w_up: bfloat16 [1536, 8960], P('dp'), may hold values from -0.15625 to 0.15625
- w_down: bfloat16 [8960, 1536], P('dp'), may hold values from -0.0625 to 0.0625
Outputs:
- block_out: bfloat16 [4, 1024, 1536], P('dp', 'ctx')
- grad_tokens: float32 [4, 1024, 1536], P('dp', 'ctx')
- grad_gain_attn: float32 [1536], P(('dp', 'ctx'))
- grad_w_qkv: float32 [1536, 2048], P(('dp', 'ctx'))
- grad_b_qkv: float32 [2048], P(('dp', 'ctx'))
- grad_w_out: float32 [1536, 1536], P(('dp', 'ctx'))
- grad_gain_mlp: float32 [1536], P(('dp', 'ctx'))
- grad_w_gate: float32 [1536, 8960], P(('dp', 'ctx'))
- grad_w_up: float32 [1536, 8960], P(('dp', 'ctx'))
- grad_w_down: float32 [8960, 1536], P(('dp', 'ctx'))
Inputs may be any that keep to these rules, and one draw needn't show every extreme that they name: A permutation in which entries 2c and 2c + 1 always add up to 15; the device of index c along ctx stores, as its first and its second 64 tokens of every sequence, that sequence's sub-blocks block_order[2c] and block_order[2c + 1]. positions[s, t] is an offset of sequence s, from 0 to 2048, plus the index idx(t) of the token stored at place t; the first sequence's offset is 0 and the last one's 2 * 1024.
All inputs are finite; a program needn't handle non-finite values.
Results may differ from a plain program's by a relative error of at most 0.02.
Values may be sent and summed in bfloat16 or wider, within the bound.
No kernel may reach another device: no remote copies, remote signals or barrier semaphores. Data moves between devices by JAX's collectives and lax.ppermute only.
A program may use at most 576 MiB of HBM per device.

v0:
```python
import math
import jax
import jax.numpy as jnp
from jax import lax
from jax.sharding import PartitionSpec as P

HEADS = 12
KV_HEADS = 2
HEAD_DIM = 128
rope_base = 1000000.0
norm_eps = 1e-06
masked_score = -1e30


def from_behind(value, axis, steps):
    count = lax.axis_size(axis)
    pairs = [(source, (source + steps) % count) for source in range(count)]
    return lax.ppermute(value, axis, pairs)


def normalize(rows_in, gain):
    inverse = lax.rsqrt(jnp.mean(rows_in * rows_in, axis=-1, keepdims=True) + norm_eps)
    normed = rows_in * inverse
    return (normed, inverse, (normed * gain.astype(jnp.float32)).astype(jnp.bfloat16))


def normalize_back(grad_out, normed, inverse, gain):
    scaled = grad_out * gain.astype(jnp.float32)
    grad_rows = inverse * (scaled - normed * jnp.mean(scaled * normed, axis=-1, keepdims=True))
    return (grad_rows, jnp.sum(grad_out * normed, axis=0))


def rope_tables(token_positions, head_dim):
    half_dim = head_dim // 2
    half_steps = jnp.arange(half_dim, dtype=jnp.float32)
    frequency = jnp.exp(-math.log(rope_base) * (2.0 * half_steps / head_dim))
    angles = token_positions.astype(jnp.float32)[:, None] * frequency[None, :]
    return (jnp.cos(angles), jnp.sin(angles))


def rotate(head_rows, cosines, sines):
    half_dim = head_rows.shape[-1] // 2
    front_half = head_rows[..., :half_dim]
    back_half = head_rows[..., half_dim:]
    cosine_part = cosines[:, None, :]
    sine_part = sines[:, None, :]
    return jnp.concatenate(
        [
            front_half * cosine_part - back_half * sine_part,
            back_half * cosine_part + front_half * sine_part,
        ],
        axis=-1,
    )


def unrotate(grad_rows, cosines, sines):
    half_dim = grad_rows.shape[-1] // 2
    front_half = grad_rows[..., :half_dim]
    back_half = grad_rows[..., half_dim:]
    cosine_part = cosines[:, None, :]
    sine_part = sines[:, None, :]
    return jnp.concatenate(
        [
            front_half * cosine_part + back_half * sine_part,
            back_half * cosine_part - front_half * sine_part,
        ],
        axis=-1,
    )


def logical_index(places, block_order, sub_len):
    slot_index = places // sub_len
    slot_match = slot_index[:, None] == jnp.arange(block_order.shape[0], dtype=jnp.int32)[None, :]
    blocks = jnp.sum(jnp.where(slot_match, block_order[None, :], 0), axis=1)
    return blocks * sub_len + places % sub_len


def block_scores(queries, key_rows, allowed, score_scale):
    scores = (
        jnp.einsum("skgtd,sukd->skgtu", queries, key_rows, preferred_element_type=jnp.float32)
        * score_scale
    )
    return jnp.where(allowed, scores, masked_score)


def attend(softmax_state, queries, kv_pair, allowed, score_scale):
    running, total_mass, summed = softmax_state
    scores = block_scores(queries, kv_pair[0], allowed, score_scale)
    newest = jnp.maximum(running, jnp.max(scores, axis=-1))
    factor = jnp.exp(running - newest)
    unscaled = jnp.exp(scores - newest[..., None])
    total_mass = total_mass * factor + jnp.sum(unscaled, axis=-1)
    summed = summed * factor[..., None] + jnp.einsum(
        "skgtu,sukd->skgtd",
        unscaled.astype(jnp.bfloat16),
        kv_pair[1],
        preferred_element_type=jnp.float32,
    )
    return (newest, total_mass, summed)


def attend_back(queries, kv_pair, allowed, log_total, grad_heads, delta, score_scale):
    scores = block_scores(queries, kv_pair[0], allowed, score_scale)
    probs_full = jnp.where(allowed, jnp.exp(scores - log_total[..., None]), 0.0)
    grad_probs = jnp.einsum(
        "skgtd,sukd->skgtu", grad_heads, kv_pair[1], preferred_element_type=jnp.float32
    )
    grad_scores = (probs_full * (grad_probs - delta[..., None])).astype(jnp.bfloat16)
    grad_query = (
        jnp.einsum("skgtu,sukd->skgtd", grad_scores, kv_pair[0], preferred_element_type=jnp.float32)
        * score_scale
    )
    grad_key = (
        jnp.einsum("skgtu,skgtd->sukd", grad_scores, queries, preferred_element_type=jnp.float32)
        * score_scale
    )
    grad_value = jnp.einsum(
        "skgtu,skgtd->sukd",
        probs_full.astype(jnp.bfloat16),
        grad_heads,
        preferred_element_type=jnp.float32,
    )
    return (grad_query, jnp.stack([grad_key, grad_value]))


def body(
    tokens,
    positions,
    block_order,
    cotangent,
    gain_attn,
    w_qkv,
    b_qkv,
    w_out,
    gain_mlp,
    w_gate,
    w_up,
    w_down,
):
    seq_count, tok_count, width = tokens.shape
    row_count = seq_count * tok_count
    ctx_count = lax.axis_size("ctx")
    ctx_place = lax.axis_index("ctx")
    groups = HEADS // KV_HEADS
    query_width = HEADS * HEAD_DIM
    kv_width = KV_HEADS * HEAD_DIM
    proj_width = query_width + 2 * kv_width
    score_scale = 1.0 / math.sqrt(HEAD_DIM)
    sub_len = tok_count // 2
    local_places = jnp.arange(tok_count, dtype=jnp.int32)
    own_index = logical_index(ctx_place * tok_count + local_places, block_order, sub_len)

    def visible(places):
        return logical_index(places, block_order, sub_len)[None, :] <= own_index[:, None]

    gain_one, qkv_full, bias_full, out_full = (
        lax.all_gather(gain_attn, "dp", axis=0, tiled=True),
        lax.all_gather(w_qkv, "dp", axis=0, tiled=True),
        lax.all_gather(b_qkv, "dp", axis=0, tiled=True),
        lax.all_gather(w_out, "dp", axis=0, tiled=True),
    )
    inputs = tokens.reshape(row_count, width).astype(jnp.float32)
    normed_one, inverse_one, hidden_one = normalize(inputs, gain_one)
    projected = jnp.dot(
        hidden_one, qkv_full, preferred_element_type=jnp.float32
    ) + bias_full.astype(jnp.float32)
    cosines, sines = rope_tables(positions.reshape(row_count), HEAD_DIM)
    query_rot = rotate(
        projected[:, :query_width].reshape(row_count, HEADS, HEAD_DIM), cosines, sines
    )
    key_rot = rotate(
        projected[:, query_width : query_width + kv_width].reshape(row_count, KV_HEADS, HEAD_DIM),
        cosines,
        sines,
    )
    value_part = projected[:, query_width + kv_width :]
    queries = (
        query_rot.astype(jnp.bfloat16)
        .reshape(seq_count, tok_count, KV_HEADS, groups, HEAD_DIM)
        .transpose(0, 2, 3, 1, 4)
    )
    key_rows = key_rot.astype(jnp.bfloat16).reshape(seq_count, tok_count, KV_HEADS, HEAD_DIM)
    value_rows = value_part.astype(jnp.bfloat16).reshape(seq_count, tok_count, KV_HEADS, HEAD_DIM)
    kv_pair = jnp.stack([key_rows, value_rows])
    start_state = (
        jnp.full((seq_count, KV_HEADS, groups, tok_count), masked_score, jnp.float32),
        jnp.zeros((seq_count, KV_HEADS, groups, tok_count), jnp.float32),
        jnp.zeros((seq_count, KV_HEADS, groups, tok_count, HEAD_DIM), jnp.float32),
    )

    def cycle_step(step_index, loop_carry):
        softmax_state, pair_now = loop_carry
        source = (ctx_place - step_index) % ctx_count
        allowed = visible(source * tok_count + local_places)
        softmax_state = attend(softmax_state, queries, pair_now, allowed, score_scale)
        pair_now = from_behind(pair_now, "ctx", 1)
        return (softmax_state, pair_now)

    softmax_state, pair_last = lax.fori_loop(0, ctx_count - 1, cycle_step, (start_state, kv_pair))
    source_last = (ctx_place - (ctx_count - 1)) % ctx_count
    softmax_state = attend(
        softmax_state,
        queries,
        pair_last,
        visible(source_last * tok_count + local_places),
        score_scale,
    )
    running, total_mass, summed = softmax_state
    attn_rows = summed / total_mass[..., None]
    log_total = running + jnp.log(total_mass)
    attn_flat = (
        attn_rows.astype(jnp.bfloat16).transpose(0, 3, 1, 2, 4).reshape(row_count, query_width)
    )
    middle = inputs + jnp.dot(attn_flat, out_full, preferred_element_type=jnp.float32)
    gain_two, gate_full, up_full, down_full = (
        lax.all_gather(gain_mlp, "dp", axis=0, tiled=True),
        lax.all_gather(w_gate, "dp", axis=0, tiled=True),
        lax.all_gather(w_up, "dp", axis=0, tiled=True),
        lax.all_gather(w_down, "dp", axis=0, tiled=True),
    )
    normed_two, inverse_two, hidden_two = normalize(middle, gain_two)
    gate_values = jnp.dot(hidden_two, gate_full, preferred_element_type=jnp.float32)
    up_values = jnp.dot(hidden_two, up_full, preferred_element_type=jnp.float32)
    sigmoid_gate = jax.nn.sigmoid(gate_values)
    activated = (gate_values * sigmoid_gate * up_values).astype(jnp.bfloat16)
    result = middle + jnp.dot(activated, down_full, preferred_element_type=jnp.float32)
    block_out = result.astype(jnp.bfloat16).reshape(seq_count, tok_count, width)
    grad_top = cotangent.reshape(row_count, width)
    gain_two_b, gate_b, up_b, down_b = (
        lax.all_gather(gain_mlp, "dp", axis=0, tiled=True),
        lax.all_gather(w_gate, "dp", axis=0, tiled=True),
        lax.all_gather(w_up, "dp", axis=0, tiled=True),
        lax.all_gather(w_down, "dp", axis=0, tiled=True),
    )
    left_part = activated
    down_share = lax.psum_scatter(
        jnp.einsum("rf,rd->fd", left_part, grad_top, preferred_element_type=jnp.float32),
        ("dp", "ctx"),
        scatter_dimension=0,
        tiled=True,
    )
    grad_act = jnp.einsum("rd,fd->rf", grad_top, down_b, preferred_element_type=jnp.float32)
    grad_gate = (
        grad_act * up_values * sigmoid_gate * (1.0 + gate_values * (1.0 - sigmoid_gate))
    ).astype(jnp.bfloat16)
    grad_up = (grad_act * gate_values * sigmoid_gate).astype(jnp.bfloat16)
    grad_gate_up = jnp.concatenate([grad_gate, grad_up], axis=1)
    left_part = hidden_two
    gate_up_share = lax.psum_scatter(
        jnp.einsum("rd,rf->df", left_part, grad_gate_up, preferred_element_type=jnp.float32),
        ("dp", "ctx"),
        scatter_dimension=0,
        tiled=True,
    )
    ff_width = gate_full.shape[1]
    gate_share = gate_up_share[:, :ff_width]
    up_share = gate_up_share[:, ff_width:]
    grad_hidden_two = jnp.einsum(
        "rf,df->rd", grad_gate, gate_b, preferred_element_type=jnp.float32
    ) + jnp.einsum("rf,df->rd", grad_up, up_b, preferred_element_type=jnp.float32)
    grad_middle_norm, grad_gain_two = normalize_back(
        grad_hidden_two, normed_two, inverse_two, gain_two_b
    )
    grad_middle = grad_top.astype(jnp.float32) + grad_middle_norm
    gain_one_b, qkv_b, bias_b, out_b = (
        lax.all_gather(gain_attn, "dp", axis=0, tiled=True),
        lax.all_gather(w_qkv, "dp", axis=0, tiled=True),
        lax.all_gather(b_qkv, "dp", axis=0, tiled=True),
        lax.all_gather(w_out, "dp", axis=0, tiled=True),
    )
    grad_branch = grad_middle.astype(jnp.bfloat16)
    grad_attn = jnp.einsum(
        "rd,qd->rq", grad_branch, out_b, preferred_element_type=jnp.float32
    ).astype(jnp.bfloat16)
    grad_heads = grad_attn.reshape(seq_count, tok_count, KV_HEADS, groups, HEAD_DIM).transpose(
        0, 2, 3, 1, 4
    )
    delta = jnp.sum(grad_heads.astype(jnp.float32) * attn_rows, axis=-1)
    zero_query = jnp.zeros((seq_count, KV_HEADS, groups, tok_count, HEAD_DIM), jnp.float32)
    zero_pair = jnp.zeros((2, seq_count, tok_count, KV_HEADS, HEAD_DIM), jnp.float32)

    def back_step(step_index, loop_carry):
        grad_query, pair_now, grad_pair = loop_carry
        source = (ctx_place - step_index) % ctx_count
        allowed = visible(source * tok_count + local_places)
        part_query, part_pair = attend_back(
            queries, pair_now, allowed, log_total, grad_heads, delta, score_scale
        )
        pair_now = from_behind(pair_now, "ctx", 1)
        grad_pair = from_behind((grad_pair + part_pair).astype(jnp.bfloat16), "ctx", 1).astype(
            jnp.float32
        )
        return (grad_query + part_query, pair_now, grad_pair)

    grad_query, pair_home, grad_pair = lax.fori_loop(
        0, ctx_count, back_step, (zero_query, kv_pair, zero_pair)
    )
    grad_query_rows = grad_query.transpose(0, 3, 1, 2, 4).reshape(row_count, HEADS, HEAD_DIM)
    grad_query_raw = unrotate(grad_query_rows, cosines, sines).reshape(row_count, query_width)
    grad_key_raw = unrotate(
        grad_pair[0].reshape(row_count, KV_HEADS, HEAD_DIM), cosines, sines
    ).reshape(row_count, kv_width)
    grad_proj = jnp.concatenate(
        [grad_query_raw, grad_key_raw, grad_pair[1].reshape(row_count, kv_width)], axis=1
    ).astype(jnp.bfloat16)
    grad_bias = jnp.sum(grad_proj.astype(jnp.float32), axis=0)
    grad_hidden_one = jnp.einsum("rc,dc->rd", grad_proj, qkv_b, preferred_element_type=jnp.float32)
    grad_input_norm, grad_gain_one = normalize_back(
        grad_hidden_one, normed_one, inverse_one, gain_one_b
    )
    grad_tokens = (grad_middle + grad_input_norm).reshape(seq_count, tok_count, width)
    attn_share = lax.psum_scatter(
        jnp.concatenate(
            [
                jnp.einsum("rd,rc->dc", hidden_one, grad_proj, preferred_element_type=jnp.float32),
                jnp.einsum("rq,rd->qd", attn_flat, grad_branch, preferred_element_type=jnp.float32),
            ],
            axis=1,
        ),
        ("dp", "ctx"),
        scatter_dimension=0,
        tiled=True,
    )
    qkv_share = attn_share[:, :proj_width]
    out_share = attn_share[:, proj_width:]
    gain_one_share, bias_share, gain_two_share = (
        lax.psum_scatter(grad_gain_one, ("dp", "ctx"), scatter_dimension=0, tiled=True),
        lax.psum_scatter(grad_bias, ("dp", "ctx"), scatter_dimension=0, tiled=True),
        lax.psum_scatter(grad_gain_two, ("dp", "ctx"), scatter_dimension=0, tiled=True),
    )
    return (
        block_out,
        grad_tokens,
        gain_one_share,
        qkv_share,
        bias_share,
        out_share,
        gain_two_share,
        gate_share,
        up_share,
        down_share,
    )


def solution(mesh):
    return jax.shard_map(
        body,
        mesh=mesh,
        in_specs=(
            P("dp", "ctx", None),
            P("dp", "ctx"),
            P(),
            P("dp", "ctx", None),
            P("dp"),
            P("dp", None),
            P("dp"),
            P("dp", None),
            P("dp"),
            P("dp", None),
            P("dp", None),
            P("dp", None),
        ),
        out_specs=(
            P("dp", "ctx", None),
            P("dp", "ctx", None),
            P(("dp", "ctx")),
            P(("dp", "ctx"), None),
            P(("dp", "ctx")),
            P(("dp", "ctx"), None),
            P(("dp", "ctx")),
            P(("dp", "ctx"), None),
            P(("dp", "ctx"), None),
            P(("dp", "ctx"), None),
        ),
        check_vma=False,
    )
```

profile of v0, /device:TPU:0, one launch (start us, length us, event | category | flops | bytes accessed | tf_op | source)
XLA Modules:
  0.0 2639.6 jit_solution(16025676978261663640)
XLA Ops:
  10.8 9.6 all-gather.2
  21.0 8.3 all-gather
  29.4 7.4 all-gather.1
  38.1 44.6 %all-gather.9.cloned.1.call-done = bf16[1536,2048]{1,0:T(8,128)(2,1)} async-done(((bf16[384,2048]{1,0:T(8,128)(2,1)}), bf16[1536,2048]{1,0:T(8,128)(2,1)}) %all-gather.9.cloned.1.call-update) | async-done | bytes 6291472 | tf_op jit(solution)/shard_map/all_gather | solution.py:158
  82.7 3.8 convolution_add_fusion.3
  93.4 44.1 %while.44 = (s32[]{:T(128)}, f32[1,2,6,128]{3,2,1,0:T(8,128)S(1)}, f32[1,2,6,128]{3,2,1,0:T(8,128)S(1)}, f32[1,2,6,128,128]{4,3,2,1,0:T(8,128)S(1)}, bf16[2,1,12...) while((s32[]{:T(128)}, f32[1,2,6,128]{3,2,1,0:T(8,128)S(1)}, ...), condition=%wide.region_6.7_spmd.clone, body=%wide.region_2.6_spmd.clone.sunk | while | flops 102664848 | bytes 5382022 | solution.py:199
  95.7 4.3 collective-permute-done
  102.0 4.3 collective-permute-done
  108.2 4.3 collective-permute-done
  114.5 4.3 collective-permute-done
  120.7 4.3 collective-permute-done
  127.0 4.3 collective-permute-done
  133.2 4.3 collective-permute-done
  141.0 2.3 fusion.94
  143.3 3.4 multiply_reduce_fusion.3
  146.9 243.6 %all-gather.15.cloned.1.call-done = bf16[1536,8960]{1,0:T(8,128)(2,1)} async-done(((bf16[384,8960]{1,0:T(8,128)(2,1)}), bf16[1536,8960]{1,0:T(8,128)(2,1)}) %all-gather.15.cloned.1.call-update) | async-done | bytes 27525136 | tf_op jit(solution)/shard_map/all_gather | solution.py:218
  390.4 15.8 fusion.96
  406.3 232.9 %all-gather.13.cloned.1.call-done = bf16[1536,8960]{1,0:T(8,128)(2,1)} async-done(((bf16[384,8960]{1,0:T(8,128)(2,1)}), bf16[1536,8960]{1,0:T(8,128)(2,1)}) %all-gather.13.cloned.1.call-update) | async-done | bytes 27525136 | tf_op jit(solution)/shard_map/all_gather | solution.py:217
  639.2 15.8 fusion.95
  655.0 232.9 %all-gather.17.cloned.1.call-done = bf16[8960,1536]{1,0:T(8,128)(2,1)} async-done(((bf16[2240,1536]{1,0:T(8,128)(2,1)}), bf16[8960,1536]{1,0:T(8,128)(2,1)}) %all-gather.17.cloned.1.call-update) | async-done | bytes 27525136 | tf_op jit(solution)/shard_map/all_gather | solution.py:219
  887.9 19.0 multiply_convert_fusion
  906.9 14.5 fusion.97
  921.4 16.0 multiply_reduce_fusion
  938.9 4.0 convolution_convert_fusion
  946.4 90.3 %while.45 = (s32[]{:T(128)}, f32[1,2,6,128,128]{4,3,2,1,0:T(8,128)S(1)}, bf16[2,1,128,2,128]{4,2,3,1,0:T(8,128)(2,1)}, f32[2,1,128,2,128]{4,2,3,1,0:T(8,128)S(1)...) while((s32[]{:T(128)}, ...), condition=%wide.region_15.16_spmd.clone, body=%wide.region_13.15_spmd.clone.sunk | while | flops 254207632 | bytes 9553853 | solution.py:295
  952.2 4.6 collective-permute-done.2
  961.9 6.2 collective-permute-done.2
  973.1 6.2 collective-permute-done.2
  984.4 6.2 collective-permute-done.2
  995.7 6.2 collective-permute-done.2
  1006.9 6.2 collective-permute-done.2
  1018.2 6.2 collective-permute-done.2
  1029.5 6.2 collective-permute-done.2
  1037.0 6.1 fusion.72
  1045.7 1.9 fusion.75
  1048.4 7.9 pad_maximum_fusion
  1057.2 50.7 %fusion.42 = f32[1536,17920]{1,0:T(8,128)} fusion(bf16[128,1536]{1,0:T(8,128)(2,1)S(1)} %copy-done.3, bf16[128,8960]{1,0:T(8,128)(2,1)} %get-tuple-element.822, bf16[128,8960]{1,0:T(8,128)(2,1)} %get-tuple-element.823), kind=kOutput, calls=%fused_computation.72 | convolution fusion | flops 7055605760 | bytes 115081216 | tf_op jit(solution)/shard_map/rd,rf->df/dot_general | solution.py:250
  1109.0 23.7 fusion.67
  1132.9 6.0 fusion.61
  1139.0 40.6 %all-reduce.4 = (f32[1536]{0:T(1024)S(1)}, f32[2048]{0:T(1024)S(1)}, f32[1536]{0:T(1024)S(1)}) all-reduce(f32[1536]{0:T(1024)S(1)} %get-tuple-element.771, f32[2048]{0:T(1024)S(1)} %convert_reduce_fusion, f32[1536]{0:T(1024)S(1)} %copy-done.18), channel_id=2, replica_groups=mesh['dp'=4,'ctx'=8] {'dp','ctx'}, use_global_device_ids=true, to_apply=%region_18.19.clone | all-reduce | flops 5120 | bytes 40960
  1181.3 2.3 fusion.60
  1183.6 15.0 fusion.47
  1198.6 81.3 %reduce-scatter.6.cloned.1.call-done = f32[48,3584]{1,0:T(8,128)} async-done(((f32[1536,3584]{1,0:T(8,128)}), f32[48,3584]{1,0:T(8,128)}) %reduce-scatter.6.cloned.1.call-update) | async-done | bytes 688144 | tf_op jit(solution)/shard_map/reduce_scatter | solution.py:312
  1279.9 1.7 slice.142
  1281.6 1.8 slice.141
  1283.3 883.2 %reduce-scatter.8.cloned.1.call-done = f32[48,17920]{1,0:T(8,128)} async-done(((f32[1536,17920]{1,0:T(8,128)}), f32[48,17920]{1,0:T(8,128)}) %reduce-scatter.8.cloned.1.call-update) | async-done | bytes 3440656 | tf_op jit(solution)/shard_map/reduce_scatter | solution.py:249
  2166.5 4.0 fusion.92
  2170.5 462.1 %reduce-scatter.10.cloned.1.call-done = f32[280,1536]{1,0:T(8,128)} async-done(((f32[8960,1536]{1,0:T(8,128)}), f32[280,1536]{1,0:T(8,128)}) %reduce-scatter.10.cloned.1.call-update) | async-done | bytes 1720336
  (345 shorter events, 82.9 us)
Async XLA Ops:
  7.2 75.5 %all-gather.9.cloned.1.call-start = ((), (), s32[]{:S(2)}) async-start(), calls=%async_computation.3 | async-start | bytes 7864320 | tf_op jit(solution)/shard_map/all_gather | solution.py:158
  7.9 135.4 %all-gather.11.cloned.1.call-start = ((), (), s32[]{:S(2)}) async-start(), calls=%async_computation.4 | async-start | bytes 5898240 | tf_op jit(solution)/shard_map/all_gather | solution.py:160
  8.7 381.8 %all-gather.15.cloned.1.call-start = ((), (), s32[]{:S(2)}) async-start(), calls=%async_computation.6 | async-start | bytes 34406400 | tf_op jit(solution)/shard_map/all_gather | solution.py:218
  9.4 629.8 %all-gather.13.cloned.1.call-start = ((), (), s32[]{:S(2)}) async-start(), calls=%async_computation.5 | async-start | bytes 34406400 | tf_op jit(solution)/shard_map/all_gather | solution.py:217
  10.0 26.9 %copy-start.24 = (s32[16]{0:T(128)S(1)}, s32[16]{0:T(128)}, u32[]{:S(2)}) copy-start(s32[16]{0:T(128)} %param.18) | copy-start | bytes 196
  10.0 27.0 %copy-start = (bf16[1,128,1536]{2,1,0:T(8,128)(2,1)S(1)}, bf16[1,128,1536]{2,1,0:T(8,128)(2,1)}, u32[]{:S(2)}) copy-start(bf16[1,128,1536]{2,1,0:T(8,128)(2,1)} %param.16) | copy-start | bytes 1179652
  10.0 27.1 %copy-start.26 = (s32[1,128]{1,0:T(1,128)S(1)}, s32[1,128]{1,0:T(1,128)}, u32[]{:S(2)}) copy-start(s32[1,128]{1,0:T(1,128)} %param.17) | copy-start | bytes 1540
  10.0 877.9 %all-gather.17.cloned.1.call-start = ((), (), s32[]{:S(2)}) async-start(), calls=%async_computation.7 | async-start | bytes 34406400 | tf_op jit(solution)/shard_map/all_gather | solution.py:219
  10.6 1269.3 %reduce-scatter.6.cloned.1.call-start = ((), (), s32[]{:S(2)}) async-start(), calls=%async_computation.8 | async-start | bytes 22708224 | tf_op jit(solution)/shard_map/reduce_scatter | solution.py:312
  29.4 53.3 %copy-start.11 = (f32[1536]{0:T(1024)}, f32[1536]{0:T(1024)S(1)}, u32[]{:S(2)}) copy-start(f32[1536]{0:T(1024)S(1)} %reshape.601) | copy-start | bytes 18436
  37.2 45.6 %copy-start.19 = (f32[128]{0:T(128)}, f32[128]{0:T(128)S(1)}, u32[]{:S(2)}) copy-start(f32[128]{0:T(128)S(1)} %add_rsqrt_fusion.1) | copy-start | bytes 1540
  37.2 45.5 %copy-start.14 = (s32[128]{0:T(128)}, s32[128]{0:T(128)S(1)}, u32[]{:S(2)}) copy-start(s32[128]{0:T(128)S(1)} %get-tuple-element.1028) | copy-start | bytes 1540
  38.1 51.6 %copy-start.7 = (f32[128,64]{0,1:T(8,128)}, f32[128,64]{0,1:T(8,128)S(1)}, u32[]{:S(2)}) copy-start(f32[128,64]{0,1:T(8,128)S(1)} %get-tuple-element.838) | copy-start | bytes 98308
  38.1 51.6 %copy-start.9 = (f32[128,64]{0,1:T(8,128)}, f32[128,64]{0,1:T(8,128)S(1)}, u32[]{:S(2)}) copy-start(f32[128,64]{0,1:T(8,128)S(1)} %get-tuple-element.839) | copy-start | bytes 98308
  93.4 45.4 %copy-start.17 = (pred[128,128]{0,1:T(8,128)(4,1)S(1)}, pred[128,128]{0,1:T(8,128)(4,1)}, u32[]{:S(2)}) copy-start(pred[128,128]{0,1:T(8,128)(4,1)} %broadcast_compare_fusion.2) | copy-start | bytes 49156
  93.8 6.2 collective-permute-start
  100.0 6.2 collective-permute-start
  106.3 6.2 collective-permute-start
  112.5 6.2 collective-permute-start
  118.8 6.2 collective-permute-start
  125.0 6.2 collective-permute-start
  131.3 6.2 collective-permute-start
  143.3 263.0 %copy-start.4 = (bf16[1,2,6,128,128]{3,4,2,1,0:T(8,128)(2,1)}, bf16[1,2,6,128,128]{3,4,2,1,0:T(8,128)(2,1)S(1)}, u32[]{:S(2)}) copy-start(bf16[1,2,6,128,128]{3,4,2,1,0:T(8,128)(2,1)S(1)} %get-tuple-element.842) | copy-start | bytes 1179652
  146.9 492.3 %copy-start.2 = (bf16[128,1536]{1,0:T(8,128)(2,1)}, bf16[128,1536]{1,0:T(8,128)(2,1)S(1)}, u32[]{:S(2)}) copy-start(bf16[128,1536]{1,0:T(8,128)(2,1)S(1)} %multiply_convert_fusion.3) | copy-start | bytes 1179652
  406.3 481.6 %copy-start.5 = (bf16[1,128,1536]{2,1,0:T(8,128)(2,1)S(1)}, bf16[1,128,1536]{2,1,0:T(8,128)(2,1)}, u32[]{:S(2)}) copy-start(bf16[1,128,1536]{2,1,0:T(8,128)(2,1)} %param.19) | copy-start | bytes 1179652
  938.9 7.5 copy-start.16
  938.9 7.5 copy-start.25
  947.4 10.3 collective-permute-start.1
  950.2 6.5 collective-permute-start.2
  958.6 10.3 collective-permute-start.1
  961.5 6.5 collective-permute-start.2
  969.9 10.3 collective-permute-start.1
  972.8 6.5 collective-permute-start.2
  981.2 10.3 collective-permute-start.1
  984.1 6.5 collective-permute-start.2
  992.4 10.3 collective-permute-start.1
  995.3 6.5 collective-permute-start.2
  1003.7 10.3 collective-permute-start.1
  1006.6 6.5 collective-permute-start.2
  1015.0 10.3 collective-permute-start.1
  1017.9 6.5 collective-permute-start.2
  1026.2 10.3 collective-permute-start.1
  1029.1 6.5 collective-permute-start.2
  1037.0 8.7 copy-start.1
  1037.0 8.7 copy-start.12
  1037.0 8.7 copy-start.20
  1056.3 1110.3 %reduce-scatter.8.cloned.1.call-start = ((), (), s32[]{:S(2)}) async-start(), calls=%async_computation.9 | async-start | bytes 113541120 | tf_op jit(solution)/shard_map/reduce_scatter | solution.py:249
  1108.0 1524.6 %reduce-scatter.10.cloned.1.call-start = ((), (), s32[]{:S(2)}) async-start(), calls=%async_computation.10 | async-start | bytes 56770560
  (13 other events, 44.9 us)
Sparse Core Ops, SparseCore 0:
  9.8 72.8 all-gather.8
  84.6 56.9 all-gather.10
  143.4 247.0 all-gather.14
  392.2 246.9 all-gather.12
  640.9 246.9 all-gather.16
  1056.4 223.4 reduce-scatter.5
  1286.3 880.1 reduce-scatter.7
  2173.5 459.0 reduce-scatter.9
where the time goes:
time: 2640 us
  waiting for transfers between devices  2260 us (86%)
  matrix products  223 us (8%)
  blocking collectives  65.9 us (2%)
  other arithmetic  40.8 us (2%)
  local copies, waits for them, and re-layouts  28.8 us (1%)
    reduce_scatter x1, waiting for transfers between devices, body(): lax.psum_scatter(jnp.einsum('rd,rf->df', left_part, grad_gate_up, preferr...  883 us
    unnamed x9, waiting for transfers between devices  465 us
    all_gather x1, waiting for transfers between devices, body(): lax.all_gather(w_up, 'dp', axis=0, tiled=True)  244 us
    all_gather x1, waiting for transfers between devices, body(): lax.all_gather(w_gate, 'dp', axis=0, tiled=True)  233 us
    all_gather x1, waiting for transfers between devices, body(): lax.all_gather(w_down, 'dp', axis=0, tiled=True)  233 us
    reduce_scatter x1, waiting for transfers between devices, body(): lax.psum_scatter(jnp.concatenate([jnp.einsum('rd,rc->dc', hidden_one, gra...  81.3 us
    ppermute x23, waiting for transfers between devices, from_behind(): return lax.ppermute(value, axis, pairs)  77.9 us
  transfers between devices with their start and end apart: 31, of which 22 were waited for; matrix products, arithmetic and copies ran while one was open for 8% of the time, Pallas kernels for 0%

commit v1 on v0

--- a/solution.py
+++ b/solution.py
@@ -1,3 +1,4 @@
+import functools
 import math
 import jax
 import jax.numpy as jnp
@@ -10,6 +11,30 @@
 rope_base = 1000000.0
 norm_eps = 1e-06
 masked_score = -1e30
+
+
+def trace_gates(target, chip_axis):
+    z_new, block_now, val2 = (
+        jax.lax.axis_size(chip_axis),
+        jax.lax.axis_index(chip_axis),
+        target.shape[0],
+    )
+    low, h_now = (target, 1)
+    while h_now < z_new:
+        low = jnp.concatenate(
+            [
+                low,
+                jax.lax.ppermute(
+                    low, chip_axis, [(no, (no - h_now) % z_new) for no in range(z_new)]
+                ),
+            ],
+            0,
+        )
+        h_now = 2 * h_now
+    return jnp.roll(low, block_now * val2, axis=0)
+
+
+pass_tails_all = functools.partial(trace_gates, chip_axis="dp")
 
 
 def from_behind(value, axis, steps):
@@ -216,7 +241,7 @@
         lax.all_gather(gain_mlp, "dp", axis=0, tiled=True),
         lax.all_gather(w_gate, "dp", axis=0, tiled=True),
         lax.all_gather(w_up, "dp", axis=0, tiled=True),
-        lax.all_gather(w_down, "dp", axis=0, tiled=True),
+        pass_tails_all(w_down),
     )
     normed_two, inverse_two, hidden_two = normalize(middle, gain_two)
     gate_values = jnp.dot(hidden_two, gate_full, preferred_element_type=jnp.float32)

time: 2640 us -> 2760 us (1.045)
  waiting for transfers between devices: 2260 us -> 2320 us
  local copies, waits for them, and re-layouts: 28.8 us -> 63.1 us
    ppermute x0 -> x2, waiting for transfers between devices: none -> 520 us  [trace_gates(): jax.lax.ppermute(low, chip_axis, [(no, (no - h_now) % z_new) for no in ra...]
    reduce_scatter x1, waiting for transfers between devices: 883 us -> 501 us  [body(): lax.psum_scatter(jnp.einsum('rd,rf->df', left_part, grad_gate_up, preferr...]
    reduce_scatter x1, waiting for transfers between devices: 81.3 us -> 0.01 us  [body(): lax.psum_scatter(jnp.concatenate([jnp.einsum('rd,rc->dc', hidden_one, gra...]
    unnamed x69 -> x118, local copies, waits for them, and re-layouts: 7.33 us -> 37.9 us
  transfers between devices with their start and end apart: 31 -> 33, of which waited for: 22 -> 24; matrix products, arithmetic and copies ran while one was open for 8% -> 9% of each run, Pallas kernels for 0% -> 0%
where the time goes in v1:
time: 2760 us; the launch traced here: 2750 us
  waiting for transfers between devices  2320 us (84%)
  matrix products  219 us (8%)
  blocking collectives  79.7 us (3%)
  local copies, waits for them, and re-layouts  63.1 us (2%)
  other arithmetic  39.8 us (1%)
    ppermute x2, waiting for transfers between devices, trace_gates(): jax.lax.ppermute(low, chip_axis, [(no, (no - h_now) % z_new) for no in ra...  520 us
    reduce_scatter x1, waiting for transfers between devices, body(): lax.psum_scatter(jnp.einsum('rd,rf->df', left_part, grad_gate_up, preferr...  501 us
    unnamed x9, waiting for transfers between devices  465 us
    all_gather x1, waiting for transfers between devices, body(): lax.all_gather(w_gate, 'dp', axis=0, tiled=True)  245 us
    all_gather x1, waiting for transfers between devices, body(): lax.all_gather(w_up, 'dp', axis=0, tiled=True)  233 us
    all_gather x1, waiting for transfers between devices, body(): lax.all_gather(w_down, 'dp', axis=0, tiled=True)  233 us
    ppermute x23, waiting for transfers between devices, from_behind(): return lax.ppermute(value, axis, pairs)  79.8 us
  transfers between devices with their start and end apart: 33, of which 24 were waited for; matrix products, arithmetic and copies ran while one was open for 9% of the time, Pallas kernels for 0%

profile of v1, /device:TPU:0, one launch (start us, length us, event | category | flops | bytes accessed | tf_op | source)
XLA Modules:
  0.0 2750.8 jit_solution(16696924188059355251)
XLA Ops:
  10.8 9.6 all-gather
  20.4 8.4 all-gather.1
  28.8 7.3 all-gather.2
  36.9 45.8 %all-gather.9.cloned.1.call-done = bf16[1536,2048]{1,0:T(8,128)(2,1)} async-done(((bf16[384,2048]{1,0:T(8,128)(2,1)}), bf16[1536,2048]{1,0:T(8,128)(2,1)}) %all-gather.9.cloned.1.call-update) | async-done | bytes 6291472 | tf_op jit(solution)/shard_map/all_gather | solution.py:183
  82.7 3.8 convolution_add_fusion.2
  90.2 44.3 %while.44 = (s32[]{:T(128)}, f32[1,2,6,128]{3,2,1,0:T(8,128)S(1)}, f32[1,2,6,128]{3,2,1,0:T(8,128)S(1)}, f32[1,2,6,128,128]{4,3,2,1,0:T(8,128)S(1)}, bf16[2,1,12...) while((s32[]{:T(128)}, f32[1,2,6,128]{3,2,1,0:T(8,128)S(1)}, ...), condition=%wide.region_6.7_spmd.clone, body=%wide.region_2.6_spmd.clone.sunk | while | flops 102664848 | bytes 5382022 | solution.py:224
  92.0 5.0 collective-permute-done
  98.2 5.0 collective-permute-done
  104.5 5.0 collective-permute-done
  110.8 5.0 collective-permute-done
  117.0 5.0 collective-permute-done
  123.3 5.0 collective-permute-done
  129.5 5.0 collective-permute-done
  145.8 244.7 %all-gather.13.cloned.1.call-done = bf16[1536,8960]{1,0:T(8,128)(2,1)} async-done(((bf16[384,8960]{1,0:T(8,128)(2,1)}), bf16[1536,8960]{1,0:T(8,128)(2,1)}) %all-gather.13.cloned.1.call-update) | async-done | bytes 27525136 | tf_op jit(solution)/shard_map/all_gather | solution.py:242
  390.4 15.8 fusion.105
  406.3 232.9 %all-gather.15.cloned.1.call-done = bf16[1536,8960]{1,0:T(8,128)(2,1)} async-done(((bf16[384,8960]{1,0:T(8,128)(2,1)}), bf16[1536,8960]{1,0:T(8,128)(2,1)}) %all-gather.15.cloned.1.call-update) | async-done | bytes 27525136 | tf_op jit(solution)/shard_map/all_gather | solution.py:243
  639.2 15.8 fusion.106
  655.0 232.9 %all-gather.17.cloned.1.call-done = bf16[8960,1536]{1,0:T(8,128)(2,1)} async-done(((bf16[2240,1536]{1,0:T(8,128)(2,1)}), bf16[8960,1536]{1,0:T(8,128)(2,1)}) %all-gather.17.cloned.1.call-update) | async-done | bytes 27525136 | tf_op jit(solution)/shard_map/all_gather | solution.py:258
  887.9 17.9 multiply_convert_fusion
  905.8 15.6 fusion.107
  921.4 16.4 multiply_reduce_fusion
  939.3 4.3 convolution_convert_fusion
  945.3 79.4 %while.45 = (s32[]{:T(128)}, f32[1,2,6,128,128]{4,3,2,1,0:T(8,128)S(1)}, bf16[2,1,128,2,128]{4,2,3,1,0:T(8,128)(2,1)S(1)}, f32[2,1,128,2,128]{4,2,3,1,0:T(8,128)...) while((s32[]{:T(128)}, ...), condition=%wide.region_15.16_spmd.clone, body=%wide.region_13.15_spmd.clone.sunk | while | flops 254207632 | bytes 9553853 | solution.py:320
  950.9 4.3 collective-permute-done.2
  959.2 5.8 collective-permute-done.2
  969.1 5.8 collective-permute-done.2
  979.0 5.8 collective-permute-done.2
  988.9 5.8 collective-permute-done.2
  998.8 5.8 collective-permute-done.2
  1008.8 5.8 collective-permute-done.2
  1018.7 5.8 collective-permute-done.2
  1025.0 5.0 fusion.81
  1034.2 7.7 pad_maximum_fusion
  1043.6 49.2 %fusion.44 = f32[1536,17920]{1,0:T(8,128)} fusion(bf16[128,1536]{1,0:T(8,128)(2,1)S(1)} %copy-done.16, bf16[128,8960]{1,0:T(8,128)(2,1)} %get-tuple-element.822, bf16[128,8960]{1,0:T(8,128)(2,1)S(1)} %copy-done.3), kind=kOutput, calls=%fused_computation.75 | convolution fusion | flops 7055605760 | bytes 115081216 | tf_op jit(solution)/shard_map/rd,rf->df/dot_general | solution.py:275
  1094.5 22.3 fusion.76
  1118.7 173.9 %collective-permute-done.3 = bf16[2240,1536]{1,0:T(8,128)(2,1)S(1)} collective-permute-done((bf16[2240,1536]{1,0:T(8,128)(2,1)}, bf16[2240,1536]{1,0:T(8,128)(2,1)S(1)}, u32[]{:S(2)}, u32[]{:S(2)}) %collective-permute-start.3) | collective-permute-done | bytes 6881312 | tf_op jit(solution)/shard_map/ppermute | solution.py:27
  1292.6 10.3 pad_maximum_fusion.1
  1304.4 6.5 constant_dynamic-update-slice_fusion.5
  1310.9 3.7 constant_dynamic-update-slice_fusion.4
  1314.7 345.8 %collective-permute-done.4 = bf16[4480,1536]{1,0:T(8,128)(2,1)} collective-permute-done((bf16[4480,1536]{1,0:T(8,128)(2,1)}, bf16[4480,1536]{1,0:T(8,128)(2,1)}, u32[]{:S(2)}, u32[]{:S(2)}) %collective-permute-start.4) | collective-permute-done | bytes 13762592 | tf_op jit(solution)/shard_map/ppermute | solution.py:27
  1660.4 13.0 constant_dynamic-update-slice_fusion.3
  1673.4 3.3 constant_dynamic-update-slice_fusion.2
  1680.1 13.7 constant_dynamic-update-slice_fusion
  1696.4 54.4 %all-reduce.4 = (f32[1536]{0:T(1024)S(1)}, f32[2048]{0:T(1024)S(1)}, f32[1536]{0:T(1024)S(1)}) all-reduce(f32[1536]{0:T(1024)S(1)} %get-tuple-element.771, f32[2048]{0:T(1024)S(1)} %convert_reduce_fusion, f32[1536]{0:T(1024)S(1)} %copy-done.35), channel_id=2, replica_groups=mesh['dp'=4,'ctx'=8] {'dp','ctx'}, use_global_device_ids=true, to_apply=%region_18.19.clone | all-reduce | flops 5120 | bytes 40960
  1753.8 19.1 fusion.54
  1776.4 501.0 %reduce-scatter.8.cloned.1.call-done = f32[48,17920]{1,0:T(8,128)} async-done(((f32[1536,17920]{1,0:T(8,128)}), f32[48,17920]{1,0:T(8,128)}) %reduce-scatter.8.cloned.1.call-update) | async-done | bytes 3440656 | tf_op jit(solution)/shard_map/reduce_scatter | solution.py:274
  2277.4 4.0 fusion.102
  2281.4 462.2 %reduce-scatter.10.cloned.1.call-done = f32[280,1536]{1,0:T(8,128)} async-done(((f32[8960,1536]{1,0:T(8,128)}), f32[280,1536]{1,0:T(8,128)}) %reduce-scatter.10.cloned.1.call-update) | async-done | bytes 1720336
  (402 shorter events, 86.8 us)
Async XLA Ops:
  7.2 75.5 %all-gather.9.cloned.1.call-start = ((), (), s32[]{:S(2)}) async-start(), calls=%async_computation.3 | async-start | bytes 7864320 | tf_op jit(solution)/shard_map/all_gather | solution.py:183
  7.9 133.6 %all-gather.11.cloned.1.call-start = ((), (), s32[]{:S(2)}) async-start(), calls=%async_computation.4 | async-start | bytes 5898240 | tf_op jit(solution)/shard_map/all_gather | solution.py:185
  8.7 381.8 %all-gather.13.cloned.1.call-start = ((), (), s32[]{:S(2)}) async-start(), calls=%async_computation.5 | async-start | bytes 34406400 | tf_op jit(solution)/shard_map/all_gather | solution.py:242
  9.4 26.9 copy-start.9
  9.4 27.1 copy-start.44
  9.5 629.7 %all-gather.15.cloned.1.call-start = ((), (), s32[]{:S(2)}) async-start(), calls=%async_computation.6 | async-start | bytes 34406400 | tf_op jit(solution)/shard_map/all_gather | solution.py:243
  10.0 877.9 %all-gather.17.cloned.1.call-start = ((), (), s32[]{:S(2)}) async-start(), calls=%async_computation.7 | async-start | bytes 34406400 | tf_op jit(solution)/shard_map/all_gather | solution.py:258
  10.6 1762.3 %reduce-scatter.6.cloned.1.call-start = ((), (), s32[]{:S(2)}) async-start(), calls=%async_computation.8 | async-start | bytes 22708224 | tf_op jit(solution)/shard_map/reduce_scatter | solution.py:337
  20.4 1010.1 %copy-start.32 = (f32[1536]{0:T(1024)}, f32[1536]{0:T(1024)S(1)}, u32[]{:S(2)}) copy-start(f32[1536]{0:T(1024)S(1)} %reshape.601) | copy-start | bytes 18436
  36.5 52.9 %copy-start.36 = (f32[128]{0:T(128)}, f32[128]{0:T(128)S(1)}, u32[]{:S(2)}) copy-start(f32[128]{0:T(128)S(1)} %add_rsqrt_fusion.1) | copy-start | bytes 1540
  36.9 52.6 %copy-start.24 = (f32[128,64]{0,1:T(8,128)}, f32[128,64]{0,1:T(8,128)S(1)}, u32[]{:S(2)}) copy-start(f32[128,64]{0,1:T(8,128)S(1)} %get-tuple-element.838) | copy-start | bytes 98308
  36.9 52.6 %copy-start.26 = (f32[128,64]{0,1:T(8,128)}, f32[128,64]{0,1:T(8,128)S(1)}, u32[]{:S(2)}) copy-start(f32[128,64]{0,1:T(8,128)S(1)} %get-tuple-element.839) | copy-start | bytes 98308
  90.7 6.2 collective-permute-start
  97.0 6.2 collective-permute-start
  103.2 6.2 collective-permute-start
  109.5 6.2 collective-permute-start
  115.7 6.2 collective-permute-start
  122.0 6.2 collective-permute-start
  128.2 6.2 collective-permute-start
  139.2 267.0 %copy-start.20 = (bf16[1,2,6,128,128]{3,4,2,1,0:T(8,128)(2,1)}, bf16[1,2,6,128,128]{3,4,2,1,0:T(8,128)(2,1)S(1)}, u32[]{:S(2)}) copy-start(bf16[1,2,6,128,128]{3,4,2,1,0:T(8,128)(2,1)S(1)} %get-tuple-element.842) | copy-start | bytes 1179652
  144.8 261.5 %copy-start.39 = (f32[128]{0:T(128)}, f32[128]{0:T(128)S(1)}, u32[]{:S(2)}) copy-start(f32[128]{0:T(128)S(1)} %add_rsqrt_fusion) | copy-start | bytes 1540
  145.8 493.4 %copy-start.15 = (bf16[128,1536]{1,0:T(8,128)(2,1)}, bf16[128,1536]{1,0:T(8,128)(2,1)S(1)}, u32[]{:S(2)}) copy-start(bf16[128,1536]{1,0:T(8,128)(2,1)S(1)} %multiply_convert_fusion.3) | copy-start | bytes 1179652
  939.3 85.6 %copy-start.7 = (f32[128,1536]{1,0:T(8,128)}, f32[128,1536]{1,0:T(8,128)S(1)}, u32[]{:S(2)}) copy-start(f32[128,1536]{1,0:T(8,128)S(1)} %multiply_add_fusion) | copy-start | bytes 2359300
  945.3 79.7 %copy-start.21 = (bf16[1,2,6,128,128]{3,4,2,1,0:T(8,128)(2,1)S(1)}, bf16[1,2,6,128,128]{3,4,2,1,0:T(8,128)(2,1)}, u32[]{:S(2)}) copy-start(bf16[1,2,6,128,128]{3,4,2,1,0:T(8,128)(2,1)} %copy-done.20) | copy-start | bytes 1179652
  945.3 9.9 collective-permute-start.1
  948.9 6.2 collective-permute-start.2
  955.2 9.9 collective-permute-start.1
  958.8 6.2 collective-permute-start.2
  965.1 9.9 collective-permute-start.1
  968.7 6.2 collective-permute-start.2
  975.0 9.9 collective-permute-start.1
  978.6 6.2 collective-permute-start.2
  984.9 9.9 collective-permute-start.1
  988.5 6.2 collective-permute-start.2
  994.8 9.9 collective-permute-start.1
  998.4 6.2 collective-permute-start.2
  1004.7 9.9 collective-permute-start.1
  1008.3 6.2 collective-permute-start.2
  1014.7 9.9 collective-permute-start.1
  1018.2 6.2 collective-permute-start.2
  1041.9 1235.5 %reduce-scatter.8.cloned.1.call-start = ((), (), s32[]{:S(2)}) async-start(), calls=%async_computation.9 | async-start | bytes 113541120 | tf_op jit(solution)/shard_map/reduce_scatter | solution.py:274
  1092.9 1650.7 %reduce-scatter.10.cloned.1.call-start = ((), (), s32[]{:S(2)}) async-start(), calls=%async_computation.10 | async-start | bytes 56770560
  1116.8 175.8 %collective-permute-start.3 = (bf16[2240,1536]{1,0:T(8,128)(2,1)}, bf16[2240,1536]{1,0:T(8,128)(2,1)S(1)}, u32[]{:S(2)}, u32[]{:S(2)}) collective-permute-start(bf16[2240,1536]{1,0:T(8,128)(2,1)} %param.27), channel_id=1, source_target_pairs={{0,24},{8,0},{16,8},{24,16},{1,25},{9,1},{17,9},{25,17},{2,26},{10... | collective-permute-start | bytes 20643848 | tf_op jit(solution)/shard_map/ppermute | solution.py:27
  1302.9 357.5 %collective-permute-start.4 = (bf16[4480,1536]{1,0:T(8,128)(2,1)}, bf16[4480,1536]{1,0:T(8,128)(2,1)}, u32[]{:S(2)}, u32[]{:S(2)}) collective-permute-start(bf16[4480,1536]{1,0:T(8,128)(2,1)} %pad_maximum_fusion.1), channel_id=1, source_target_pairs={{0,16},{8,24},{16,0},{24,8},{1,17},{9,25},{17,1},{25,9},{2,18},{10... | collective-permute-start | bytes 41287688 | tf_op jit(solution)/shard_map/ppermute | solution.py:27
  1310.9 362.5 %slice-start = ((s8[6881280]{0:T(1024)(128)(4,1)}), s8[4194304]{0:T(1024)(128)(4,1)S(1)}, s32[]{:S(2)}) async-start(s8[6881280]{0:T(1024)(128)(4,1)} %bitcast.261), calls=%async_computation.11 | async-start | bytes 8388608
  1314.6 358.8 %slice-start.1 = ((s8[6881280]{0:T(1024)(128)(4,1)}), s8[2686976]{0:T(1024)(128)(4,1)S(1)}, s32[]{:S(2)}) async-start(s8[6881280]{0:T(1024)(128)(4,1)} %bitcast.261), calls=%async_computation.12 | async-start | bytes 5373952
  1693.8 58.8 %copy-start.8 = (f32[128,1536]{1,0:T(8,128)S(1)}, f32[128,1536]{1,0:T(8,128)}, u32[]{:S(2)}) copy-start(f32[128,1536]{1,0:T(8,128)} %copy-done.7) | copy-start | bytes 2359300
  1693.8 59.9 %copy-start.6 = (f32[128,1536]{1,0:T(8,128)S(1)}, f32[128,1536]{1,0:T(8,128)}, u32[]{:S(2)}) copy-start(f32[128,1536]{1,0:T(8,128)} %copy-done.4) | copy-start | bytes 2359300
  (37 other events, 308.7 us)
Sparse Core Ops, SparseCore 0:
  9.8 72.8 all-gather.8
  84.5 56.9 all-gather.10
  143.4 247.0 all-gather.12
  392.1 246.9 all-gather.14
  640.9 246.9 all-gather.16
  1042.1 354.5 reduce-scatter.5
  1403.0 874.3 reduce-scatter.7
  2284.4 459.0 reduce-scatter.9
